TPU v7x, 512 devices: a whole 4x8x8 slice. The times are simulated.
512 devices in a mesh: blk: 32 (over x_lo, y, core), tm: 16 (over z, x_hi).
Axes of the slice: x: 4 (x_hi: 2, x_lo: 2; x = x_hi * 2 + x_lo), y: 8, z: 8, core: 2. Of those that a mesh axis runs over, the one named last changes fastest.
Arguments:
- clips: bfloat16 [32, 32, 16, 36, 256], P('blk', 'tm'), may hold values from -6 to 6
- cotangent: bfloat16 [32, 32, 16, 36, 256], P('blk', 'tm'), may hold values from -6 to 6
- conv_master: float32 [3072, 256], P('blk'), may hold values from -0.125 to 0.125
- first_moment: float32 [3072, 256], P('blk'), may hold values from -3 to 3
- second_moment: float32 [3072, 256], P('blk'), may hold values from 0.1 to 100
- norm_gain: float32 [256], replicated, may hold values from 0.5 to 1.5
- norm_bias: float32 [256], replicated, may hold values from -3 to 3
Outputs:
- block_out: bfloat16 [32, 32, 16, 36, 256], P('blk', 'tm')
- input_grad: bfloat16 [32, 32, 16, 36, 256], P('blk', 'tm')
- new_master: float32 [3072, 256], P('blk')
- new_first: float32 [3072, 256], P('blk')
- new_second: float32 [3072, 256], P('blk')
- norm_grads: float32 [2, 256], replicated
All inputs are finite; a program needn't handle non-finite values.
Results may differ from a plain program's by a relative error of at most 0.0063.
Values may be sent and summed in bfloat16 or wider, within the bound.
A program may use at most 64 MiB of HBM per device.

v0:
```python
import jax
import jax.numpy as jnp
from jax import lax
from jax.sharding import PartitionSpec as P

GROUPS = 32
beta_one = 0.9
beta_two = 0.999
learn_rate = 0.003
adam_eps = 1e-08
bias_first = 1.0 - 0.9**10
bias_second = 1.0 - 0.999**10


def extended(block, sides, width):
    for axis, dim in sides:
        count = lax.axis_size(axis)
        forward = [(i, i + 1) for i in range(count - 1)]
        backward = [(target, source) for source, target in forward]
        low = lax.ppermute(
            lax.slice_in_dim(block, block.shape[dim] - width, None, axis=dim), axis, forward
        )
        high = lax.ppermute(lax.slice_in_dim(block, 0, width, axis=dim), axis, backward)
        block = jnp.concatenate([low, block, high], axis=dim)
    return block


def norm_act(field, gain, bias):
    shape = field.shape
    grouped = field.reshape(shape[:-3] + (shape[-3] * shape[-2], GROUPS, shape[-1] // GROUPS))
    center = jnp.mean(grouped, axis=(-3, -1), keepdims=True)
    spread = jnp.mean((grouped - center) ** 2, axis=(-3, -1), keepdims=True)
    normed = ((grouped - center) * lax.rsqrt(spread + 1e-05)).reshape(shape)
    return jax.nn.silu(normed * gain + bias)


def adam_update(gradient, master, first, second):
    new_first = beta_one * first + (1.0 - beta_one) * gradient
    new_second = beta_two * second + (1.0 - beta_two) * gradient * gradient
    update = new_first / bias_first / (jnp.sqrt(new_second / bias_second) + adam_eps)
    return (master - learn_rate * update, new_first, new_second)


def shards(clips, cotangent, conv_master, first_moment, second_moment, norm_gain, norm_bias):
    f32 = jnp.float32
    frames, height, width, channels = (
        clips.shape[1],
        clips.shape[2],
        clips.shape[3],
        clips.shape[4],
    )
    weights = lax.all_gather(conv_master.astype(jnp.bfloat16), "blk", axis=0, tiled=True)
    inputs32 = clips.astype(f32)
    act32, pullback = jax.vjp(norm_act, inputs32, norm_gain, norm_bias)
    act = act32.astype(jnp.bfloat16)
    act_padded = jnp.pad(act, ((0, 0), (0, 0), (1, 1), (1, 1), (0, 0)))
    space32 = jnp.zeros(clips.shape, f32)
    for row_tap in range(3):
        for col_tap in range(3):
            tap_index = 3 * row_tap + col_tap
            window = act_padded[:, :, row_tap : row_tap + height, col_tap : col_tap + width, :]
            tap = weights[tap_index * channels : (tap_index + 1) * channels]
            space32 = space32 + jnp.einsum(
                "bfhwc,cd->bfhwd", window, tap, preferred_element_type=f32
            )
    space = space32.astype(jnp.bfloat16)
    space_padded = extended(space, (("tm", 1),), 1)
    temporal = jnp.zeros(clips.shape, f32)
    for frame_tap in range(3):
        tap = weights[(9 + frame_tap) * channels : (10 + frame_tap) * channels]
        temporal = temporal + jnp.einsum(
            "bfhwc,cd->bfhwd",
            space_padded[:, frame_tap : frame_tap + frames],
            tap,
            preferred_element_type=f32,
        )
    block_out = (inputs32 + temporal).astype(jnp.bfloat16)
    back_weights = lax.all_gather(conv_master.astype(jnp.bfloat16), "blk", axis=0, tiled=True)
    grad_padded = extended(cotangent, (("tm", 1),), 1)
    space_grad32 = jnp.zeros(clips.shape, f32)
    temporal_grads = []
    for frame_tap in range(3):
        tap = back_weights[(9 + frame_tap) * channels : (10 + frame_tap) * channels]
        space_grad32 = space_grad32 + jnp.einsum(
            "bfhwd,cd->bfhwc",
            grad_padded[:, 2 - frame_tap : 2 - frame_tap + frames],
            tap,
            preferred_element_type=f32,
        )
        temporal_grads.append(
            jnp.einsum(
                "bfhwc,bfhwd->cd",
                space_padded[:, frame_tap : frame_tap + frames],
                cotangent,
                preferred_element_type=f32,
            )
        )
    space_grad = space_grad32.astype(jnp.bfloat16)
    sgrad_padded = jnp.pad(space_grad, ((0, 0), (0, 0), (1, 1), (1, 1), (0, 0)))
    act_grad = jnp.zeros(clips.shape, f32)
    spatial_grads = []
    for row_tap in range(3):
        for col_tap in range(3):
            tap_index = 3 * row_tap + col_tap
            tap = back_weights[tap_index * channels : (tap_index + 1) * channels]
            window = act_padded[:, :, row_tap : row_tap + height, col_tap : col_tap + width, :]
            spatial_grads.append(
                jnp.einsum("bfhwc,bfhwd->cd", window, space_grad, preferred_element_type=f32)
            )
            back_window = sgrad_padded[
                :, :, 2 - row_tap : 2 - row_tap + height, 2 - col_tap : 2 - col_tap + width, :
            ]
            act_grad = act_grad + jnp.einsum(
                "bfhwd,cd->bfhwc", back_window, tap, preferred_element_type=f32
            )
    input_term, gain_grad, bias_grad = pullback(act_grad)
    input_grad = (cotangent.astype(f32) + input_term).astype(jnp.bfloat16)
    local_gradient = jnp.concatenate(spatial_grads + temporal_grads, axis=0)
    norm_grads = lax.psum(jnp.stack([gain_grad, bias_grad]), ("blk", "tm"))
    row_block = lax.psum_scatter(local_gradient, "blk", scatter_dimension=0, tiled=True)
    gradient = lax.psum(row_block, "tm")
    new_master, new_first, new_second = adam_update(
        gradient, conv_master, first_moment, second_moment
    )
    return (block_out, input_grad, new_master, new_first, new_second, norm_grads)


def solution(mesh):
    placed = (
        P("blk", "tm", None, None, None),
        P("blk", "tm", None, None, None),
        P("blk", None),
        P("blk", None),
        P("blk", None),
        P(),
        P(),
    )
    return jax.shard_map(
        shards,
        mesh=mesh,
        in_specs=placed,
        out_specs=(
            P("blk", "tm", None, None, None),
            P("blk", "tm", None, None, None),
            P("blk", None),
            P("blk", None),
            P("blk", None),
            P(),
        ),
        check_vma=False,
    )
```

profile of v0, /device:TPU:8, one launch (start us, length us, event | category | flops | bytes accessed | tf_op | source)
XLA Modules:
  0.0 426.8 jit_solution(4757618439813596500)
XLA Ops:
  7.2 1.5 convert_element_type.38
  8.8 1.3 copy.26
  10.1 0.8 fusion.179
  10.9 4.9 %collective-permute-start.3 = (bf16[1,1,16,36,256]{4,3,2,1,0:T(8,128)(2,1)S(1)}, bf16[1,1,16,36,256]{4,3,2,1,0:T(8,128)(2,1)S(1)}, u32[]{:S(2)}, u32[]{:S(2)}) collective-permute-start(bf16[1,1,16,36,256]{4,3,2,1,0:T(8,128)(2,1)S(1)} %get-tuple-element.25), channel_id=1, source_target_pairs={{0,1},{1,2},{2,3},{3,4},{4,5},{5,6},{6,7},{7,8},{8,9},{9,10},{10,1... | collective-permute-start | bytes 884744 | tf_op jit(solution)/shard_map/ppermute | solution.py:20
  15.8 1.3 collective-permute-start.2
  17.1 0.2 convert_reduce_fusion
  17.7 0.3 fusion.17
  18.2 0.1 mul.163
  18.3 11.4 %collective-permute-done.3 = bf16[1,1,16,36,256]{4,3,2,1,0:T(8,128)(2,1)S(1)} collective-permute-done((bf16[1,1,16,36,256]{4,3,2,1,0:T(8,128)(2,1)S(1)}, bf16[1,1,16,36,256]{4,3,2,1,0:T(8,128)(2,1)S(1)}, u32[]{:S(2)}, u32[]{:S(2)}) %collective-permute-start.3) | collective-permute-done | bytes 294944 | tf_op jit(solution)/shard_map/ppermute | solution.py:20
  29.8 0.7 copy-done.12
  30.5 50.4 %all-gather.2.cloned.1.call-done = bf16[3072,256]{1,0:T(8,128)(2,1)} async-done(((bf16[96,256]{1,0:T(8,128)(2,1)}), bf16[3072,256]{1,0:T(8,128)(2,1)}) %all-gather.2.cloned.1.call-update) | async-done | bytes 1572880 | tf_op jit(solution)/shard_map/all_gather | solution.py:52
  80.9 1.5 fusion.51
  82.5 0.4 fusion.114
  82.9 1.4 fusion.9
  84.3 0.4 fusion.66
  84.7 0.4 convolution_add_fusion.7
  85.1 0.4 convolution_add_fusion.6
  85.5 0.4 convolution_add_fusion.5
  85.9 0.4 convolution_add_fusion.4
  86.3 0.4 convolution_add_fusion.3
  86.7 0.4 convolution_add_fusion.2
  87.1 0.4 convolution_add_fusion.1
  87.5 0.3 copy-done.15
  87.8 1.2 fusion.26
  89.0 1.1 copy-done.5
  90.1 0.5 fusion.37
  91.0 0.1 mul.188
  91.1 0.3 fusion.4
  91.7 3.0 fusion.14
  94.7 1.1 fusion.49
  95.8 1.1 fusion.48
  96.9 1.1 fusion.47
  98.0 1.1 fusion.46
  99.1 1.1 fusion.45
  100.2 1.1 fusion.44
  101.3 1.1 fusion.43
  102.4 0.4 fusion.85
  102.8 0.4 convolution_add_fusion.17
  103.1 0.4 convolution_add_fusion.16
  103.5 0.4 convolution_add_fusion.15
  103.9 0.3 convolution_add_fusion.14
  104.2 0.4 convolution_add_fusion.13
  104.6 0.4 convolution_add_fusion.12
  105.0 0.5 convolution_add_fusion.11
  105.5 0.4 fusion.10
  106.0 5.0 %collective-permute-start = (bf16[1,1,16,36,256]{4,3,2,1,0:T(8,128)(2,1)S(1)}, bf16[1,1,16,36,256]{4,3,2,1,0:T(8,128)(2,1)S(1)}, u32[]{:S(2)}, u32[]{:S(2)}) collective-permute-start(bf16[1,1,16,36,256]{4,3,2,1,0:T(8,128)(2,1)S(1)} %get-tuple-element.26), channel_id=1, source_target_pairs={{0,1},{1,2},{2,3},{3,4},{4,5},{5,6},{6,7},{7,8},{8,9},{9,10},{10,1... | collective-permute-start | bytes 884744 | tf_op jit(solution)/shard_map/ppermute | solution.py:20
  111.0 1.1 fusion.42
  112.1 1.4 collective-permute-start.1
  113.5 1.1 fusion.41
  114.6 10.7 %collective-permute-done = bf16[1,1,16,36,256]{4,3,2,1,0:T(8,128)(2,1)S(1)} collective-permute-done((bf16[1,1,16,36,256]{4,3,2,1,0:T(8,128)(2,1)S(1)}, bf16[1,1,16,36,256]{4,3,2,1,0:T(8,128)(2,1)S(1)}, u32[]{:S(2)}, u32[]{:S(2)}) %collective-permute-start) | collective-permute-done | bytes 294944 | tf_op jit(solution)/shard_map/ppermute | solution.py:20
  125.3 1.2 fusion.40
  126.5 1.1 fusion.39
  127.7 0.7 copy-done.10
  128.4 1.2 fusion.38
  129.7 1.0 copy-done.6
  130.7 0.9 copy.36
  131.7 98.4 %psum.15 = f32[2,256]{1,0:T(2,128)} all-reduce(f32[2,256]{1,0:T(2,128)S(1)} %pad_maximum_fusion.4), channel_id=1, replica_groups=mesh['blk'=32,'tm'=16] {'blk','tm'}, use_global_device_ids=true, to_apply=%region_14.15 | all-reduce | flops 512 | bytes 4096 | tf_op jit(solution)/shard_map/psum | solution.py:119
  230.1 1.4 fusion.129
  231.6 1.4 fusion.127
  233.0 19.1 %reduce-scatter.2.cloned.1.call-done = f32[96,256]{1,0:T(8,128)} async-done(((f32[3072,256]{1,0:T(8,128)}), f32[96,256]{1,0:T(8,128)}) %reduce-scatter.2.cloned.1.call-update) | async-done | bytes 98320 | tf_op jit(solution)/shard_map/reduce_scatter | solution.py:120
  252.1 2.2 fusion.11
  254.4 0.9 copy.35
  255.3 163.4 %all-reduce.4.cloned.1.call-done = f32[96,256]{1,0:T(8,128)} async-done(((f32[96,256]{1,0:T(8,128)}), f32[96,256]{1,0:T(8,128)}) %all-reduce.4.cloned.1.call-update) | async-done | bytes 98320 | tf_op jit(solution)/shard_map/psum | solution.py:121
  418.7 1.6 multiply_subtract_fusion
  (59 shorter events, 1.8 us)
Async XLA Ops:
  7.2 73.8 %all-gather.2.cloned.1.call-start = ((), (), s32[]{:S(2)}) async-start(), calls=%async_computation.1 | async-start | bytes 1622016 | tf_op jit(solution)/shard_map/all_gather | solution.py:52
  8.7 8.4 %copy-start = (bf16[1,2,16,36,256]{4,2,3,1,0:T(8,128)(2,1)S(1)}, bf16[1,2,16,36,256]{4,2,3,1,0:T(8,128)(2,1)}, u32[]{:S(2)}) copy-start(bf16[1,2,16,36,256]{4,2,3,1,0:T(8,128)(2,1)} %param.7) | copy-start | bytes 1769476
  8.8 243.3 %reduce-scatter.2.cloned.1.call-start = ((), (), s32[]{:S(2)}) async-start(), calls=%async_computation.2 | async-start | bytes 3244032 | tf_op jit(solution)/shard_map/reduce_scatter | solution.py:120
  10.9 18.9 %collective-permute-start.3 = (bf16[1,1,16,36,256]{4,3,2,1,0:T(8,128)(2,1)S(1)}, bf16[1,1,16,36,256]{4,3,2,1,0:T(8,128)(2,1)S(1)}, u32[]{:S(2)}, u32[]{:S(2)}) collective-permute-start(bf16[1,1,16,36,256]{4,3,2,1,0:T(8,128)(2,1)S(1)} %get-tuple-element.25), channel_id=1, source_target_pairs={{0,1},{1,2},{2,3},{3,4},{4,5},{5,6},{6,7},{7,8},{8,9},{9,10},{10,1... | collective-permute-start | bytes 884744 | tf_op jit(solution)/shard_map/ppermute | solution.py:20
  15.8 67.1 %collective-permute-start.2 = (bf16[1,1,16,36,256]{4,3,2,1,0:T(8,128)(2,1)}, bf16[1,1,16,36,256]{4,3,2,1,0:T(8,128)(2,1)}, u32[]{:S(2)}, u32[]{:S(2)}) collective-permute-start(bf16[1,1,16,36,256]{4,3,2,1,0:T(8,128)(2,1)} %get-tuple-element.24), channel_id=1, source_target_pairs={{1,0},{2,1},{3,2},{4,3},{5,4},{6,5},{7,6},{8,7},{9,8},{10,9},{11,1... | collective-permute-start | bytes 884744 | tf_op jit(solution)/shard_map/ppermute | solution.py:23
  17.9 64.5 %copy-start.2 = (bf16[1,2,16,36,256]{4,2,3,1,0:T(8,128)(2,1)S(1)}, bf16[1,2,16,36,256]{4,2,3,1,0:T(8,128)(2,1)}, u32[]{:S(2)}) copy-start(bf16[1,2,16,36,256]{4,2,3,1,0:T(8,128)(2,1)} %param.8) | copy-start | bytes 1769476
  29.8 0.7 copy-start.12
  80.9 1.6 copy-start.1
  87.1 0.7 copy-start.15
  87.1 0.7 copy-start.16
  89.0 1.1 copy-start.5
  90.1 1.7 copy-start.3
  106.0 19.3 %collective-permute-start = (bf16[1,1,16,36,256]{4,3,2,1,0:T(8,128)(2,1)S(1)}, bf16[1,1,16,36,256]{4,3,2,1,0:T(8,128)(2,1)S(1)}, u32[]{:S(2)}, u32[]{:S(2)}) collective-permute-start(bf16[1,1,16,36,256]{4,3,2,1,0:T(8,128)(2,1)S(1)} %get-tuple-element.26), channel_id=1, source_target_pairs={{0,1},{1,2},{2,3},{3,4},{4,5},{5,6},{6,7},{7,8},{8,9},{9,10},{10,1... | collective-permute-start | bytes 884744 | tf_op jit(solution)/shard_map/ppermute | solution.py:20
  112.1 13.3 %copy-start.4 = (bf16[1,2,16,36,256]{4,2,3,1,0:T(8,128)(2,1)S(1)}, bf16[1,2,16,36,256]{4,2,3,1,0:T(8,128)(2,1)}, u32[]{:S(2)}) copy-start(bf16[1,2,16,36,256]{4,2,3,1,0:T(8,128)(2,1)} %param.8) | copy-start | bytes 1769476
  112.1 15.6 %collective-permute-start.1 = (bf16[1,1,16,36,256]{4,3,2,1,0:T(8,128)(2,1)S(1)}, bf16[1,1,16,36,256]{4,3,2,1,0:T(8,128)(2,1)S(1)}, u32[]{:S(2)}, u32[]{:S(2)}) collective-permute-start(bf16[1,1,16,36,256]{4,3,2,1,0:T(8,128)(2,1)S(1)} %get-tuple-element.27), channel_id=1, source_target_pairs={{1,0},{2,1},{3,2},{4,3},{5,4},{6,5},{7,6},{8,7},{9,8},{10,9},{11,1... | collective-permute-start | bytes 884744 | tf_op jit(solution)/shard_map/ppermute | solution.py:23
  125.3 1.2 copy-start.8
  127.7 0.7 copy-start.10
  129.7 1.1 copy-start.6
  129.7 289.0 %all-reduce.4.cloned.1.call-start = ((), (), s32[]{:S(2)}) async-start(), calls=%async_computation.3 | async-start | bytes 196608 | tf_op jit(solution)/shard_map/psum | solution.py:121
  131.7 99.9 %copy-start.11 = (bf16[1,1,16,36,256]{4,3,2,1,0:T(8,128)(2,1)S(1)}, bf16[1,1,16,36,256]{4,3,2,1,0:T(8,128)(2,1)}, u32[]{:S(2)}) copy-start(bf16[1,1,16,36,256]{4,3,2,1,0:T(8,128)(2,1)} %copy-done.10) | copy-start | bytes 884740
  231.6 20.5 %copy-start.9 = (bf16[1,1,16,36,256]{4,3,2,1,0:T(8,128)(2,1)S(1)}, bf16[1,1,16,36,256]{4,3,2,1,0:T(8,128)(2,1)}, u32[]{:S(2)}) copy-start(bf16[1,1,16,36,256]{4,3,2,1,0:T(8,128)(2,1)} %copy-done.8) | copy-start | bytes 884740
  254.3 164.3 %copy-start.7 = (f32[96,256]{1,0:T(8,128)S(1)}, f32[96,256]{1,0:T(8,128)}, u32[]{:S(2)}) copy-start(f32[96,256]{1,0:T(8,128)} %param.9) | copy-start | bytes 294916
  254.3 164.3 %copy-start.13 = (f32[96,256]{1,0:T(8,128)S(1)}, f32[96,256]{1,0:T(8,128)}, u32[]{:S(2)}) copy-start(f32[96,256]{1,0:T(8,128)} %param.10) | copy-start | bytes 294916
  254.4 164.3 %copy-start.14 = (f32[96,256]{1,0:T(8,128)S(1)}, f32[96,256]{1,0:T(8,128)}, u32[]{:S(2)}) copy-start(f32[96,256]{1,0:T(8,128)} %param.11) | copy-start | bytes 294916
Sparse Core Ops, SparseCore 0:
  10.7 70.1 all-gather.1
  129.8 122.2 reduce-scatter.1
  255.0 163.6 all-reduce.3
where the time goes:
time: 427 us
  waiting for transfers between devices  255 us (60%)
  blocking collectives  98.4 us (23%)
  matrix products  29.6 us (7%)
  between operations  14.1 us (3%)
  starting transfers between devices  12.7 us (3%)
  local copies, waits for them, and re-layouts  9.06 us (2%)
  other arithmetic  7.8 us (2%)
    psum x1, waiting for transfers between devices, shards(): gradient = lax.psum(row_block, 'tm')  163 us
    psum x1, blocking collectives, shards(): norm_grads = lax.psum(jnp.stack([gain_grad, bias_grad]), ('blk', 'tm'))  98.4 us
    all_gather x1, waiting for transfers between devices, shards(): lax.all_gather(conv_master.astype(jnp.bfloat16), 'blk', axis=0, tiled=True)  50.4 us
    ppermute x2, waiting for transfers between devices, extended(): lax.ppermute(lax.slice_in_dim(block, block.shape[dim] - width, None, axis...  22.2 us
    reduce_scatter x1, waiting for transfers between devices, shards(): lax.psum_scatter(local_gradient, 'blk', scatter_dimension=0, tiled=True)  19.1 us
    ppermute x2, starting transfers between devices, extended(): lax.ppermute(lax.slice_in_dim(block, block.shape[dim] - width, None, axis...  9.9 us
    dot_general x9, matrix products, shards(): jnp.einsum('bfhwc,bfhwd->cd', window, space_grad, preferred_element_type=...  9.86 us
  transfers between devices with their start and end apart: 7, of which 5 were waited for; matrix products, arithmetic and copies ran while one was open for 4% of the time, Pallas kernels for 0%

commit v1 on v0

--- a/solution.py
+++ b/solution.py
@@ -49,7 +49,12 @@
         clips.shape[3],
         clips.shape[4],
     )
-    weights = lax.all_gather(conv_master.astype(jnp.bfloat16), "blk", axis=0, tiled=True)
+    weights = jnp.concatenate(
+        lax.all_to_all(
+            jnp.stack([conv_master.astype(jnp.bfloat16)] * lax.axis_size("blk")), "blk", 0, 0
+        ),
+        axis=0,
+    )
     inputs32 = clips.astype(f32)
     act32, pullback = jax.vjp(norm_act, inputs32, norm_gain, norm_bias)
     act = act32.astype(jnp.bfloat16)

time: 427 us -> 442 us (1.035)
  matrix products: 29.6 us -> 38.6 us
  starting transfers between devices: 12.7 us -> 20.6 us
    dot_general x9, matrix products: 3.51 us -> 11.6 us  [shards(): jnp.einsum('bfhwc,cd->bfhwd', window, tap, preferred_element_type=f32)]
    all_to_all x0 -> x1, starting transfers between devices: none -> 7.91 us  [shards(): lax.all_to_all(jnp.stack([conv_master.astype(jnp.bfloat16)] * lax.axis_si...]
    ppermute x2, waiting for transfers between devices: 22.2 us -> 14.7 us  [extended(): lax.ppermute(lax.slice_in_dim(block, block.shape[dim] - width, None, axis...]
    all_gather x1, waiting for transfers between devices: 50.4 us -> 56.7 us  [shards(): lax.all_gather(conv_master.astype(jnp.bfloat16), 'blk', axis=0, tiled=True)]
  transfers between devices with their start and end apart: 7 -> 8, of which waited for: 5 -> 5; matrix products, arithmetic and copies ran while one was open for 4% -> 8% of each run, Pallas kernels for 0% -> 0%
where the time goes in v1:
time: 442 us
  waiting for transfers between devices  251 us (57%)
  blocking collectives  101 us (23%)
  matrix products  38.6 us (9%)
  starting transfers between devices  20.6 us (5%)
  between operations  14.1 us (3%)
  local copies, waits for them, and re-layouts  8.91 us (2%)
  other arithmetic  7.82 us (2%)
    psum x1, waiting for transfers between devices, shards(): gradient = lax.psum(row_block, 'tm')  164 us
    psum x1, blocking collectives, shards(): norm_grads = lax.psum(jnp.stack([gain_grad, bias_grad]), ('blk', 'tm'))  101 us
    all_gather x1, waiting for transfers between devices, shards(): lax.all_gather(conv_master.astype(jnp.bfloat16), 'blk', axis=0, tiled=True)  56.7 us
    reduce_scatter x1, waiting for transfers between devices, shards(): lax.psum_scatter(local_gradient, 'blk', scatter_dimension=0, tiled=True)  15.8 us
    ppermute x2, waiting for transfers between devices, extended(): lax.ppermute(lax.slice_in_dim(block, block.shape[dim] - width, None, axis...  14.7 us
    dot_general x9, matrix products, shards(): jnp.einsum('bfhwc,cd->bfhwd', window, tap, preferred_element_type=f32)  11.6 us
    ppermute x2, starting transfers between devices, extended(): lax.ppermute(lax.slice_in_dim(block, block.shape[dim] - width, None, axis...  10 us
    dot_general x9, matrix products, shards(): jnp.einsum('bfhwc,bfhwd->cd', window, space_grad, preferred_element_type=...  9.84 us
  transfers between devices with their start and end apart: 8, of which 5 were waited for; matrix products, arithmetic and copies ran while one was open for 8% of the time, Pallas kernels for 0%

profile of v1, /device:TPU:8, one launch (start us, length us, event | category | flops | bytes accessed | tf_op | source)
XLA Modules:
  0.0 441.5 jit_solution(12793911782159635749)
XLA Ops:
  7.2 1.5 convert_element_type.38
  8.8 1.3 copy.26
  10.1 4.9 %collective-permute-start.3 = (bf16[1,1,16,36,256]{4,3,2,1,0:T(8,128)(2,1)S(1)}, bf16[1,1,16,36,256]{4,3,2,1,0:T(8,128)(2,1)S(1)}, u32[]{:S(2)}, u32[]{:S(2)}) collective-permute-start(bf16[1,1,16,36,256]{4,3,2,1,0:T(8,128)(2,1)S(1)} %get-tuple-element.25), channel_id=1, source_target_pairs={{0,1},{1,2},{2,3},{3,4},{4,5},{5,6},{6,7},{7,8},{8,9},{9,10},{10,1... | collective-permute-start | bytes 884744 | tf_op jit(solution)/shard_map/ppermute | solution.py:20
  15.0 1.3 collective-permute-start.2
  16.3 1.4 stack.8
  17.7 7.9 %all-to-all-start = ((bf16[32,96,256]{2,1,0:T(8,128)(2,1)}), bf16[32,96,256]{2,1,0:T(8,128)(2,1)}, u32[]{:S(2)}, u32[]{:S(2)}) async-start(bf16[32,96,256]{2,1,0:T(8,128)(2,1)} %stack.8), calls=%async_computation | async-start | bytes 3145728 | tf_op jit(solution)/shard_map/all_to_all | solution.py:53
  25.7 0.2 convert_reduce_fusion
  26.2 0.3 fusion.17
  26.8 0.1 mul.163
  26.9 3.9 collective-permute-done.3
  30.8 56.7 %all-gather.2.cloned.1.call-done = bf16[3072,256]{1,0:T(8,128)(2,1)} async-done(((bf16[96,256]{1,0:T(8,128)(2,1)}), bf16[3072,256]{1,0:T(8,128)(2,1)}) %all-gather.2.cloned.1.call-update) | async-done | bytes 1572880 | tf_op jit(solution)/shard_map/all_gather | solution.py:83
  87.5 1.4 fusion.51
  88.9 0.4 fusion.114
  89.4 0.4 fusion.9
  89.8 0.4 fusion.66
  90.2 0.4 convolution_add_fusion.7
  90.6 0.4 convolution_add_fusion.6
  91.0 0.4 convolution_add_fusion.5
  91.4 0.4 convolution_add_fusion.4
  91.8 0.4 convolution_add_fusion.3
  92.2 0.4 convolution_add_fusion.2
  92.6 0.4 convolution_add_fusion.1
  93.0 0.3 copy-done.11
  93.3 1.2 fusion.26
  94.5 1.1 copy-done.2
  95.6 0.5 fusion.37
  96.5 0.1 mul.188
  96.6 0.3 fusion.4
  97.2 3.0 fusion.14
  100.3 1.1 fusion.49
  101.3 1.1 fusion.48
  102.4 1.1 fusion.47
  103.5 1.1 fusion.46
  104.6 1.1 fusion.45
  105.7 1.1 fusion.44
  106.8 1.1 fusion.43
  107.9 1.3 fusion.85
  109.2 1.2 convolution_add_fusion.17
  110.4 1.3 convolution_add_fusion.16
  111.7 1.3 convolution_add_fusion.15
  113.0 1.2 convolution_add_fusion.14
  114.2 1.3 convolution_add_fusion.13
  115.5 1.3 convolution_add_fusion.12
  116.8 1.4 convolution_add_fusion.11
  118.2 1.3 fusion.10
  119.6 5.1 %collective-permute-start = (bf16[1,1,16,36,256]{4,3,2,1,0:T(8,128)(2,1)S(1)}, bf16[1,1,16,36,256]{4,3,2,1,0:T(8,128)(2,1)S(1)}, u32[]{:S(2)}, u32[]{:S(2)}) collective-permute-start(bf16[1,1,16,36,256]{4,3,2,1,0:T(8,128)(2,1)S(1)} %get-tuple-element.26), channel_id=1, source_target_pairs={{0,1},{1,2},{2,3},{3,4},{4,5},{5,6},{6,7},{7,8},{8,9},{9,10},{10,1... | collective-permute-start | bytes 884744 | tf_op jit(solution)/shard_map/ppermute | solution.py:20
  124.6 1.1 fusion.42
  125.7 1.3 collective-permute-start.1
  127.0 1.1 fusion.41
  128.1 10.8 %collective-permute-done = bf16[1,1,16,36,256]{4,3,2,1,0:T(8,128)(2,1)S(1)} collective-permute-done((bf16[1,1,16,36,256]{4,3,2,1,0:T(8,128)(2,1)S(1)}, bf16[1,1,16,36,256]{4,3,2,1,0:T(8,128)(2,1)S(1)}, u32[]{:S(2)}, u32[]{:S(2)}) %collective-permute-start) | collective-permute-done | bytes 294944 | tf_op jit(solution)/shard_map/ppermute | solution.py:20
  139.0 1.2 fusion.40
  140.2 1.1 fusion.39
  141.3 0.7 copy-done.7
  142.1 1.2 fusion.38
  143.4 1.0 copy-done.3
  144.4 0.9 copy.36
  145.3 100.5 %psum.15 = f32[2,256]{1,0:T(2,128)} all-reduce(f32[2,256]{1,0:T(2,128)S(1)} %pad_maximum_fusion.4), channel_id=1, replica_groups=mesh['blk'=32,'tm'=16] {'blk','tm'}, use_global_device_ids=true, to_apply=%region_14.15 | all-reduce | flops 512 | bytes 4096 | tf_op jit(solution)/shard_map/psum | solution.py:124
  245.8 2.4 fusion.129
  248.2 2.4 fusion.127
  250.6 15.8 %reduce-scatter.2.cloned.1.call-done = f32[96,256]{1,0:T(8,128)} async-done(((f32[3072,256]{1,0:T(8,128)}), f32[96,256]{1,0:T(8,128)}) %reduce-scatter.2.cloned.1.call-update) | async-done | bytes 98320 | tf_op jit(solution)/shard_map/reduce_scatter | solution.py:125
  266.4 2.3 fusion.11
  268.7 0.9 copy.35
  269.6 163.8 %all-reduce.4.cloned.1.call-done = f32[96,256]{1,0:T(8,128)} async-done(((f32[96,256]{1,0:T(8,128)}), f32[96,256]{1,0:T(8,128)}) %all-reduce.4.cloned.1.call-update) | async-done | bytes 98320 | tf_op jit(solution)/shard_map/psum | solution.py:126
  433.4 1.6 multiply_subtract_fusion
  (54 shorter events, 1.8 us)
Async XLA Ops:
  7.2 80.3 %all-gather.2.cloned.1.call-start = ((), (), s32[]{:S(2)}) async-start(), calls=%async_computation.2 | async-start | bytes 1622016 | tf_op jit(solution)/shard_map/all_gather | solution.py:83
  8.7 7.6 %copy-start.5 = (bf16[96,256]{1,0:T(8,128)(2,1)S(1)}, bf16[96,256]{1,0:T(8,128)(2,1)}, u32[]{:S(2)}) copy-start(bf16[96,256]{1,0:T(8,128)(2,1)} %convert_element_type.38) | copy-start | bytes 147460
  10.1 20.7 %collective-permute-start.3 = (bf16[1,1,16,36,256]{4,3,2,1,0:T(8,128)(2,1)S(1)}, bf16[1,1,16,36,256]{4,3,2,1,0:T(8,128)(2,1)S(1)}, u32[]{:S(2)}, u32[]{:S(2)}) collective-permute-start(bf16[1,1,16,36,256]{4,3,2,1,0:T(8,128)(2,1)S(1)} %get-tuple-element.25), channel_id=1, source_target_pairs={{0,1},{1,2},{2,3},{3,4},{4,5},{5,6},{6,7},{7,8},{8,9},{9,10},{10,1... | collective-permute-start | bytes 884744 | tf_op jit(solution)/shard_map/ppermute | solution.py:20
  15.0 74.3 %collective-permute-start.2 = (bf16[1,1,16,36,256]{4,3,2,1,0:T(8,128)(2,1)S(1)}, bf16[1,1,16,36,256]{4,3,2,1,0:T(8,128)(2,1)S(1)}, u32[]{:S(2)}, u32[]{:S(2)}) collective-permute-start(bf16[1,1,16,36,256]{4,3,2,1,0:T(8,128)(2,1)S(1)} %get-tuple-element.24), channel_id=1, source_target_pairs={{1,0},{2,1},{3,2},{4,3},{5,4},{6,5},{7,6},{8,7},{9,8},{10,9},{11,1... | collective-permute-start | bytes 884744 | tf_op jit(solution)/shard_map/ppermute | solution.py:23
  17.7 8.0 %copy-start = (bf16[1,2,16,36,256]{4,2,3,1,0:T(8,128)(2,1)S(1)}, bf16[1,2,16,36,256]{4,2,3,1,0:T(8,128)(2,1)}, u32[]{:S(2)}) copy-start(bf16[1,2,16,36,256]{4,2,3,1,0:T(8,128)(2,1)} %param.7) | copy-start | bytes 1769476
  17.7 90.2 %all-to-all-start = ((bf16[32,96,256]{2,1,0:T(8,128)(2,1)}), bf16[32,96,256]{2,1,0:T(8,128)(2,1)}, u32[]{:S(2)}, u32[]{:S(2)}) async-start(bf16[32,96,256]{2,1,0:T(8,128)(2,1)} %stack.8), calls=%async_computation | async-start | bytes 3145728 | tf_op jit(solution)/shard_map/all_to_all | solution.py:53
  25.6 240.7 %reduce-scatter.2.cloned.1.call-start = ((), (), s32[]{:S(2)}) async-start(), calls=%async_computation.3 | async-start | bytes 3244032 | tf_op jit(solution)/shard_map/reduce_scatter | solution.py:125
  26.5 62.4 %copy-start.1 = (bf16[1,2,16,36,256]{4,2,3,1,0:T(8,128)(2,1)S(1)}, bf16[1,2,16,36,256]{4,2,3,1,0:T(8,128)(2,1)}, u32[]{:S(2)}) copy-start(bf16[1,2,16,36,256]{4,2,3,1,0:T(8,128)(2,1)} %param.8) | copy-start | bytes 1769476
  87.5 1.5 copy-start.4
  92.6 0.7 copy-start.11
  92.6 0.7 copy-start.12
  94.5 1.1 copy-start.2
  119.6 19.4 %collective-permute-start = (bf16[1,1,16,36,256]{4,3,2,1,0:T(8,128)(2,1)S(1)}, bf16[1,1,16,36,256]{4,3,2,1,0:T(8,128)(2,1)S(1)}, u32[]{:S(2)}, u32[]{:S(2)}) collective-permute-start(bf16[1,1,16,36,256]{4,3,2,1,0:T(8,128)(2,1)S(1)} %get-tuple-element.26), channel_id=1, source_target_pairs={{0,1},{1,2},{2,3},{3,4},{4,5},{5,6},{6,7},{7,8},{8,9},{9,10},{10,1... | collective-permute-start | bytes 884744 | tf_op jit(solution)/shard_map/ppermute | solution.py:20
  125.7 15.6 %collective-permute-start.1 = (bf16[1,1,16,36,256]{4,3,2,1,0:T(8,128)(2,1)S(1)}, bf16[1,1,16,36,256]{4,3,2,1,0:T(8,128)(2,1)S(1)}, u32[]{:S(2)}, u32[]{:S(2)}) collective-permute-start(bf16[1,1,16,36,256]{4,3,2,1,0:T(8,128)(2,1)S(1)} %get-tuple-element.27), channel_id=1, source_target_pairs={{1,0},{2,1},{3,2},{4,3},{5,4},{6,5},{7,6},{8,7},{9,8},{10,9},{11,1... | collective-permute-start | bytes 884744 | tf_op jit(solution)/shard_map/ppermute | solution.py:23
  141.3 0.7 copy-start.7
  143.3 1.1 copy-start.3
  143.3 290.0 %all-reduce.4.cloned.1.call-start = ((), (), s32[]{:S(2)}) async-start(), calls=%async_computation.4 | async-start | bytes 196608 | tf_op jit(solution)/shard_map/psum | solution.py:126
  145.3 102.9 %copy-start.8 = (bf16[1,1,16,36,256]{4,3,2,1,0:T(8,128)(2,1)S(1)}, bf16[1,1,16,36,256]{4,3,2,1,0:T(8,128)(2,1)}, u32[]{:S(2)}) copy-start(bf16[1,1,16,36,256]{4,3,2,1,0:T(8,128)(2,1)} %copy-done.7) | copy-start | bytes 884740
  268.6 164.7 %copy-start.6 = (f32[96,256]{1,0:T(8,128)S(1)}, f32[96,256]{1,0:T(8,128)}, u32[]{:S(2)}) copy-start(f32[96,256]{1,0:T(8,128)} %param.9) | copy-start | bytes 294916
  268.6 164.7 %copy-start.9 = (f32[96,256]{1,0:T(8,128)S(1)}, f32[96,256]{1,0:T(8,128)}, u32[]{:S(2)}) copy-start(f32[96,256]{1,0:T(8,128)} %param.10) | copy-start | bytes 294916
  268.7 164.7 %copy-start.10 = (f32[96,256]{1,0:T(8,128)S(1)}, f32[96,256]{1,0:T(8,128)}, u32[]{:S(2)}) copy-start(f32[96,256]{1,0:T(8,128)} %param.11) | copy-start | bytes 294916
Sparse Core Ops, SparseCore 0:
  10.7 76.7 all-gather.1
  143.4 122.8 reduce-scatter.1
  269.2 164.0 all-reduce.3
